TPU v7x, 32 devices: a whole 2x2x4 slice. The times are simulated.
32 devices in a mesh: gx: 8 (over z, x), gy: 2 (over y), pa: 2 (over core).
Axes of the slice: x: 2, y: 2, z: 4, core: 2. Of those that a mesh axis runs over, the one named last changes fastest.
Arguments:
- leaf_maps: bfloat16 [8, 2, 2, 1024, 1024], P('gx', 'gy', None, 'pa'), may hold values from -0.125 to 0.125
- face_index: int32 [8, 2, 1024], P('gx', 'gy'), may hold values from 0 to 1023, each once within a row
- order_x: int32 [4, 2], replicated, may hold values from 0 to 1
- order_y: int32 [4, 1], replicated, may hold values from 0 to 1
- traces: float32 [8, 2, 2, 1024], P('gx', 'gy'), may hold values from -6 to 6
Outputs:
- merged_map: bfloat16 [8, 2, 2, 2, 128, 1024], P('gx', 'gy', 'pa')
- outgoing: float32 [8, 2, 2, 2, 128], P('gx', 'gy', 'pa')
Inputs may be any that keep to these rules, and one draw needn't show every extreme that they name: `face_index`: each row is a permutation of 0 to 1023.
All inputs are finite; a program needn't handle non-finite values.
Results may differ from a plain program's by a relative error of at most 0.0058.
Values may be sent and summed in bfloat16 or wider, within the bound.
A program may use at most 64 MiB of HBM per device.

v0:
```python
import jax
import jax.numpy as jnp
from jax import lax
from jax.sharding import PartitionSpec as P


def from_partner(value, axis, apart):
    mask = 2**apart
    pairs = [(source, source ^ mask) for source in range(lax.axis_size(axis))]
    return lax.ppermute(value, axis, pairs)


def complex_rows(left_block, right_block):
    real_part = jnp.dot(
        left_block[0], right_block[0], preferred_element_type=jnp.float32
    ) - jnp.dot(left_block[1], right_block[1], preferred_element_type=jnp.float32)
    imag_part = jnp.dot(
        left_block[0], right_block[1], preferred_element_type=jnp.float32
    ) + jnp.dot(left_block[1], right_block[0], preferred_element_type=jnp.float32)
    return (real_part, imag_part)


def folder(left_rows, segment):
    real_part, imag_part = complex_rows(left_rows, segment)
    return (real_part, imag_part)


def per_device(leaf_maps, face_index, order_x, order_y, traces):
    own_panel = jnp.take(leaf_maps[0, 0], face_index[0, 0], axis=2)
    panel_rows = own_panel.shape[1]
    width = own_panel.shape[2]
    half_rows = panel_rows // 2
    quarter = panel_rows // 4
    half_index = lax.axis_index("gx") % 2
    vert_index = lax.axis_index("gy") % 2
    pair_index = lax.axis_index("gx") // 2
    column_index = lax.axis_index("gy")
    first_bit = order_x[pair_index, column_index]
    sibling = from_partner(own_panel, "gx", 0)
    right_panel = jnp.where(half_index == first_bit, own_panel, sibling)
    left_panel = jnp.where(half_index == first_bit, sibling, own_panel)
    left_rows = lax.dynamic_slice_in_dim(left_panel, half_index * half_rows, half_rows, 1)
    blocks = lax.all_to_all(left_rows, "pa", split_axis=2, concat_axis=1, tiled=True)
    real_part, imag_part = complex_rows(blocks, right_panel)
    summed = lax.psum_scatter(
        jnp.concatenate([real_part, imag_part], axis=1), "pa", scatter_dimension=0, tiled=True
    )
    real_one = summed[:, :width]
    imag_one = summed[:, width:]
    merged_one = jnp.stack([real_one, imag_one]).astype(jnp.bfloat16)
    second_bit = order_y[pair_index, column_index // 2]
    other_box = from_partner(merged_one, "gy", 0)
    right_two = jnp.where(vert_index == second_bit, merged_one, other_box)
    left_two = jnp.where(vert_index == second_bit, other_box, merged_one)
    left_rows_two = lax.dynamic_slice_in_dim(left_two, vert_index * quarter, quarter, 1)
    other_half = from_partner(right_two, "gx", 0)
    first_part = jnp.where(half_index == 0, right_two, other_half)
    second_part = jnp.where(half_index == 0, other_half, right_two)
    full_panel = jnp.concatenate([first_part, second_part], axis=1)
    real_two, imag_two = folder(left_rows_two, lax.all_gather(full_panel, "pa", axis=1, tiled=True))
    merged_two = jnp.stack([real_two, imag_two]).astype(jnp.bfloat16)
    trace_sum = traces[0, 0] + from_partner(traces[0, 0], "gx", 0)
    trace_sum = trace_sum + from_partner(trace_sum, "gy", 0)
    wide = merged_two.astype(jnp.float32)
    highest = lax.Precision.HIGHEST
    real_out = jnp.dot(wide[0], trace_sum[0], precision=highest) - jnp.dot(
        wide[1], trace_sum[1], precision=highest
    )
    imag_out = jnp.dot(wide[0], trace_sum[1], precision=highest) + jnp.dot(
        wide[1], trace_sum[0], precision=highest
    )
    outgoing = jnp.stack([real_out, imag_out]).reshape(1, 1, 1, 2, quarter)
    return (merged_two.reshape(1, 1, 1, 2, quarter, width), outgoing)


def solution(mesh):
    placed = (
        P("gx", "gy", None, "pa", None),
        P("gx", "gy", None),
        P(),
        P(),
        P("gx", "gy", None, None),
    )
    return jax.shard_map(
        per_device,
        mesh=mesh,
        in_specs=placed,
        out_specs=(P("gx", "gy", "pa", None, None, None), P("gx", "gy", "pa", None, None)),
        check_vma=False,
    )
```

profile of v0, /device:TPU:0, one launch (start us, length us, event | category | flops | bytes accessed | tf_op | source)
XLA Modules:
  0.0 207.1 jit_solution(6228542808558593444)
XLA Ops:
  7.2 6.2 %copy.9 = bf16[1,1,2,512,1024]{3,2,4,1,0:T(2,128)(2,1)} copy(bf16[1,1,2,512,1024]{4,3,2,1,0:T(8,128)(2,1)} %param.5) | data formatting | bytes 4194304 | tf_op args[0]
  13.4 7.5 %gather_fusion = bf16[1024,2,512]{2,1,0:T(2,128)(2,1)S(1)} fusion(bf16[2,512,1024]{1,0,2:T(2,128)(2,1)} %bitcast.99, s32[1024]{0:T(1024)S(1)} %broadcast_clamp_fusion), kind=kCustom, calls=%fused_computation | custom fusion | bytes 4198400 | tf_op jit(solution)/shard_map/jit(_take)/gather | solution.py:29
  20.9 4.6 %fusion = bf16[2,512,1024]{1,0,2:T(2,128)(2,1)} fusion(bf16[1024,2,512]{2,1,0:T(2,128)(2,1)S(1)} %gather_fusion, pred[1024]{0:T(1024)(128)(4,1)S(1)} %compare_and_fusion), kind=kLoop, calls=%fused_computation.7 | loop fusion | flops 1048576 | bytes 4195328 | tf_op jit(solution)/shard_map/jit(_take)/select_n | solution.py:29
  25.5 3.0 %collective-permute-start = (bf16[2,512,1024]{1,0,2:T(2,128)(2,1)}, bf16[2,512,1024]{1,0,2:T(2,128)(2,1)}, u32[]{:S(2)}, u32[]{:S(2)}) collective-permute-start(bf16[2,512,1024]{1,0,2:T(2,128)(2,1)} %fusion), channel_id=1, source_target_pairs={{0,4},{4,0},{8,12},{12,8},{16,20},{20,16},{24,28},{28,24},{1,5},{5... | collective-permute-start | bytes 6291464 | tf_op jit(solution)/shard_map/ppermute | solution.py:10
  29.7 44.7 %collective-permute-done = bf16[2,512,1024]{1,0,2:T(2,128)(2,1)} collective-permute-done((bf16[2,512,1024]{1,0,2:T(2,128)(2,1)}, bf16[2,512,1024]{1,0,2:T(2,128)(2,1)}, u32[]{:S(2)}, u32[]{:S(2)}) %collective-permute-start) | collective-permute-done | bytes 2097184 | tf_op jit(solution)/shard_map/ppermute | solution.py:10
  74.4 2.6 %broadcast_select_fusion.2 = bf16[2,256,1024]{1,0,2:T(2,128)(2,1)S(1)} fusion(pred[]{:T(512)S(6)} %eq.16, bf16[2,512,1024]{1,0,2:T(2,128)(2,1)} %fusion, s32[]{:T(128)S(6)} %select_n.95, bf16[2,512,1024]{1,0,2:T(2,128)(2,1)} %collective-permute-done), kind=kLoop, calls=%fused_computation.8 | loop fusion | flops 524288 | bytes 3145733 | tf_op jit(solution)/shard_map/jit(_where)/select_n | solution.py:41
  77.0 5.4 %all_to_all.15 = bf16[2,256,1024]{1,0,2:T(2,128)(2,1)} all-to-all(bf16[2,256,1024]{1,0,2:T(2,128)(2,1)S(1)} %broadcast_select_fusion.2), channel_id=1, replica_groups=mesh['gx'=8,'gy'=2,'pa'=2] {'pa'}, dimensions={2} | all-to-all | bytes 2097152 | tf_op jit(solution)/shard_map/all_to_all | solution.py:43
  82.4 2.4 %copy.10 = bf16[2,256,2,512]{3,1,2,0:T(8,128)(2,1)S(1)} copy(bf16[2,256,2,512]{1,0,3,2:T(2,128)(2,1)} %bitcast.105) | data formatting | bytes 2097152 | tf_op jit(solution)/shard_map/all_to_all | solution.py:43
  85.9 6.0 %broadcast_select_fusion.1 = bf16[2,512,1024]{1,0,2:T(2,128)(2,1)S(1)} fusion(bf16[2,512,1024]{1,0,2:T(2,128)(2,1)} %collective-permute-done, pred[]{:T(512)S(6)} %eq.16, bf16[1024,2,512]{2,1,0:T(2,128)(2,1)S(1)} %gather_fusion, pred[1024]{0:T(1024)(128)(4,1)S(1)} %compare_and_fusion), kind=kLoop, calls=%fused_computation.3 | loop fusion | flops 2097152 | bytes 6292481 | tf_op jit(solution)/shard_map/jit(_where)/select_n | solution.py:40
  91.9 3.8 %fusion.21 = (bf16[1,512,1024]{1,0,2:T(2,128)(2,1)}, bf16[1,512,1024]{1,0,2:T(2,128)(2,1)S(1)}) fusion(bf16[2,512,1024]{1,0,2:T(2,128)(2,1)S(1)} %broadcast_select_fusion.1), kind=kLoop, calls=%fused_computation.55 | loop fusion | bytes 4194304 | tf_op jit(solution)/shard_map/slice | solution.py:16
  95.7 2.6 %copy.11 = bf16[1,512,1024]{2,1,0:T(8,128)(2,1)S(1)} copy(bf16[1,512,1024]{1,0,2:T(2,128)(2,1)S(1)} %get-tuple-element.5) | data formatting | bytes 2097152 | tf_op jit(solution)/shard_map/slice | solution.py:15
  98.3 4.6 %copy.12 = bf16[1,512,1024]{2,1,0:T(8,128)(2,1)S(1)} copy(bf16[1,512,1024]{1,0,2:T(2,128)(2,1)} %get-tuple-element.4) | data formatting | bytes 2097152 | tf_op jit(solution)/shard_map/slice | solution.py:16
  106.2 2.5 %pad_maximum_fusion = f32[512,2048]{1,0:T(8,128)} fusion(f32[512,1024]{1,0:T(8,128)S(1)} %convolution_add_fusion, f32[512,1024]{1,0:T(8,128)S(1)} %convolution_subtract_fusion), kind=kLoop, calls=%fused_computation.1 | loop fusion | flops 1048576 | bytes 8388608 | tf_op jit(solution)/shard_map/concatenate | solution.py:46
  108.7 13.6 %reduce-scatter.2.cloned.1.call-done = f32[256,2048]{1,0:T(8,128)} async-done(((f32[512,2048]{1,0:T(8,128)}), f32[256,2048]{1,0:T(8,128)}) %reduce-scatter.2.cloned.1.call-update) | async-done | bytes 2097168 | tf_op jit(solution)/shard_map/reduce_scatter | solution.py:45
  122.3 1.7 convert.20
  124.3 1.9 collective-permute-start.1
  127.4 22.3 %collective-permute-done.1 = bf16[2,256,1024]{2,1,0:T(8,128)(2,1)S(1)} collective-permute-done((bf16[2,256,1024]{2,1,0:T(8,128)(2,1)S(1)}, bf16[2,256,1024]{2,1,0:T(8,128)(2,1)S(1)}, u32[]{:S(2)}, u32[]{:S(2)}) %collective-permute-start.1) | collective-permute-done | bytes 1048608 | tf_op jit(solution)/shard_map/ppermute | solution.py:10
  149.9 1.8 collective-permute-start.2
  151.6 23.0 %collective-permute-done.2 = bf16[2,256,1024]{2,1,0:T(8,128)(2,1)} collective-permute-done((bf16[2,256,1024]{2,1,0:T(8,128)(2,1)S(1)}, bf16[2,256,1024]{2,1,0:T(8,128)(2,1)}, u32[]{:S(2)}, u32[]{:S(2)}) %collective-permute-start.2) | collective-permute-done | bytes 1048608 | tf_op jit(solution)/shard_map/ppermute | solution.py:10
  179.8 2.1 %collective-permute-done.3 = f32[2,1024]{1,0:T(2,128)S(1)} collective-permute-done((f32[2,1024]{1,0:T(2,128)S(1)}, f32[2,1024]{1,0:T(2,128)S(1)}, u32[]{:S(2)}, u32[]{:S(2)}) %collective-permute-start.3) | collective-permute-done | bytes 8224 | tf_op jit(solution)/shard_map/ppermute | solution.py:10
  183.5 2.1 %collective-permute-done.4 = f32[2,1024]{1,0:T(2,128)S(1)} collective-permute-done((f32[2,1024]{1,0:T(2,128)S(1)}, f32[2,1024]{1,0:T(2,128)S(1)}, u32[]{:S(2)}, u32[]{:S(2)}) %collective-permute-start.4) | collective-permute-done | bytes 8224 | tf_op jit(solution)/shard_map/ppermute | solution.py:10
  185.8 6.5 %all-gather.2.cloned.1.call-done = bf16[2,1024,1024]{2,1,0:T(8,128)(2,1)} async-done(((bf16[2,512,1024]{2,1,0:T(8,128)(2,1)}), bf16[2,1024,1024]{2,1,0:T(8,128)(2,1)}) %all-gather.2.cloned.1.call-update) | async-done | bytes 4194320 | tf_op jit(solution)/shard_map/all_gather | solution.py:60
  192.4 2.2 %fusion.1 = f32[128,1024]{1,0:T(8,128)S(1)} fusion(bf16[2,1024,1024]{2,1,0:T(8,128)(2,1)} %all-gather.2.cloned.1.call-done, bf16[2,128,1024]{2,1,0:T(8,128)(2,1)S(1)} %fusion.20), kind=kOutput, calls=%fused_computation.9 | convolution fusion | flops 268435456 | bytes 2883584 | tf_op jit(solution)/shard_map/dot_general | solution.py:19
  194.6 2.1 fusion.8
  (46 shorter events, 16.4 us)
Async XLA Ops:
  7.2 119.0 %copy-start = (s32[4,1]{0,1:T(1,128)S(1)}, s32[4,1]{0,1:T(1,128)}, u32[]{:S(2)}) copy-start(s32[4,1]{0,1:T(1,128)} %param.8) | copy-start | bytes 52
  7.2 6.2 %copy-start.3 = (s32[1,1,1024]{2,1,0:T(1,128)S(1)}, s32[1,1,1024]{2,1,0:T(1,128)}, u32[]{:S(2)}) copy-start(s32[1,1,1024]{2,1,0:T(1,128)} %param.6) | copy-start | bytes 12292
  7.2 115.2 %reduce-scatter.2.cloned.1.call-start = ((), (), s32[]{:S(2)}) async-start(), calls=%async_computation.2 | async-start | bytes 6291456 | tf_op jit(solution)/shard_map/reduce_scatter | solution.py:45
  20.9 7.6 %copy-start.5 = (s32[4,2]{0,1:T(2,128)S(1)}, s32[4,2]{0,1:T(2,128)}, u32[]{:S(2)}) copy-start(s32[4,2]{0,1:T(2,128)} %param.7) | copy-start | bytes 100
  25.5 48.9 %collective-permute-start = (bf16[2,512,1024]{1,0,2:T(2,128)(2,1)}, bf16[2,512,1024]{1,0,2:T(2,128)(2,1)}, u32[]{:S(2)}, u32[]{:S(2)}) collective-permute-start(bf16[2,512,1024]{1,0,2:T(2,128)(2,1)} %fusion), channel_id=1, source_target_pairs={{0,4},{4,0},{8,12},{12,8},{16,20},{20,16},{24,28},{28,24},{1,5},{5... | collective-permute-start | bytes 6291464 | tf_op jit(solution)/shard_map/ppermute | solution.py:10
  98.3 4.6 %copy-start.1 = (bf16[1,2,256,512]{3,2,1,0:T(8,128)(2,1)S(1)}, bf16[1,2,256,512]{3,2,1,0:T(8,128)(2,1)}, u32[]{:S(2)}) copy-start(bf16[1,2,256,512]{3,2,1,0:T(8,128)(2,1)} %get-tuple-element.9) | copy-start | bytes 1572868
  103.7 1.0 copy-start.2
  108.7 83.7 %all-gather.2.cloned.1.call-start = ((), (), s32[]{:S(2)}) async-start(), calls=%async_computation.3 | async-start | bytes 6291456 | tf_op jit(solution)/shard_map/all_gather | solution.py:60
  124.3 25.5 %collective-permute-start.1 = (bf16[2,256,1024]{2,1,0:T(8,128)(2,1)S(1)}, bf16[2,256,1024]{2,1,0:T(8,128)(2,1)S(1)}, u32[]{:S(2)}, u32[]{:S(2)}) collective-permute-start(bf16[2,256,1024]{2,1,0:T(8,128)(2,1)S(1)} %pad_maximum_fusion.2), channel_id=1, source_target_pairs={{0,2},{2,0},{1,3},{3,1},{4,6},{6,4},{5,7},{7,5},{8,10},{10,8},{9,1... | collective-permute-start | bytes 3145736 | tf_op jit(solution)/shard_map/ppermute | solution.py:10
  149.9 24.7 %collective-permute-start.2 = (bf16[2,256,1024]{2,1,0:T(8,128)(2,1)S(1)}, bf16[2,256,1024]{2,1,0:T(8,128)(2,1)}, u32[]{:S(2)}, u32[]{:S(2)}) collective-permute-start(bf16[2,256,1024]{2,1,0:T(8,128)(2,1)S(1)} %broadcast_select_fusion.5), channel_id=1, source_target_pairs={{0,4},{4,0},{8,12},{12,8},{16,20},{20,16},{24,28},{28,24},{1,5},{5... | collective-permute-start | bytes 3145736 | tf_op jit(solution)/shard_map/ppermute | solution.py:10
  177.6 0.7 copy-start.4
  178.3 3.7 %collective-permute-start.3 = (f32[2,1024]{1,0:T(2,128)S(1)}, f32[2,1024]{1,0:T(2,128)S(1)}, u32[]{:S(2)}, u32[]{:S(2)}) collective-permute-start(f32[2,1024]{1,0:T(2,128)S(1)} %bitcast.110), channel_id=1, source_target_pairs={{0,4},{4,0},{8,12},{12,8},{16,20},{20,16},{24,28},{28,24},{1,5},{5... | collective-permute-start | bytes 24584 | tf_op jit(solution)/shard_map/ppermute | solution.py:10
  182.0 3.7 %collective-permute-start.4 = (f32[2,1024]{1,0:T(2,128)S(1)}, f32[2,1024]{1,0:T(2,128)S(1)}, u32[]{:S(2)}, u32[]{:S(2)}) collective-permute-start(f32[2,1024]{1,0:T(2,128)S(1)} %bitcast_add_fusion), channel_id=1, source_target_pairs={{0,2},{2,0},{1,3},{3,1},{4,6},{6,4},{5,7},{7,5},{8,10},{10,8},{9,1... | collective-permute-start | bytes 24584 | tf_op jit(solution)/shard_map/ppermute | solution.py:10
  192.4 4.9 %copy-start.6 = (bf16[2,1024,1024]{2,1,0:T(8,128)(2,1)S(1)}, bf16[2,1024,1024]{2,1,0:T(8,128)(2,1)}, u32[]{:S(2)}) copy-start(bf16[2,1024,1024]{2,1,0:T(8,128)(2,1)} %all-gather.2.cloned.1.call-done) | copy-start | bytes 12582916
Sparse Core Ops, SparseCore 0:
  108.8 13.5 reduce-scatter.1
  177.8 14.5 all-gather.1
where the time goes:
time: 208 us; the launch traced here: 207 us
  waiting for transfers between devices  114 us (55%)
  local copies, waits for them, and re-layouts  30.4 us (15%)
  other arithmetic  22.3 us (11%)
  between operations  15.6 us (8%)
  starting transfers between devices  9.77 us (5%)
  matrix products  9.28 us (4%)
  blocking collectives  5.37 us (3%)
    ppermute x5, waiting for transfers between devices, from_partner(): return lax.ppermute(value, axis, pairs)  94.2 us
    reduce_scatter x1, waiting for transfers between devices, per_device(): lax.psum_scatter(jnp.concatenate([real_part, imag_part], axis=1), 'pa', s...  13.6 us
    ppermute x5, starting transfers between devices, from_partner(): return lax.ppermute(value, axis, pairs)  9.69 us
    slice x2, local copies, waits for them, and re-layouts, complex_rows(): right_block[1]  8.47 us
    gather x1, local copies, waits for them, and re-layouts, per_device(): own_panel = jnp.take(leaf_maps[0, 0], face_index[0, 0], axis=2)  7.46 us
    unnamed x15, local copies, waits for them, and re-layouts  7.18 us
    all_gather x1, waiting for transfers between devices, per_device(): lax.all_gather(full_panel, 'pa', axis=1, tiled=True)  6.55 us
    select_n x1, other arithmetic, per_device(): right_panel = jnp.where(half_index == first_bit, own_panel, sibling)  5.96 us
  transfers between devices with their start and end apart: 7, of which 7 were waited for; matrix products, arithmetic and copies ran while one was open for 1% of the time, Pallas kernels for 0%

commit v1 on v0

v1 whole, which is shorter than its diff:
```python
import functools

import jax
import jax.numpy as jnp
from jax import lax
from jax.experimental import pallas as pl
from jax.experimental.pallas import tpu as pltpu
from jax.sharding import PartitionSpec as P

MESH = pl.DeviceIdType.MESH
CHUNKS = 4


def one_hot(index_row, size):
    rows = lax.broadcasted_iota(jnp.int32, (size, index_row.shape[1]), 0)
    return (rows == index_row).astype(jnp.float32).astype(jnp.bfloat16)


def kernel(
    role_ref, leaf_ref, index_ref, trace_ref, map_ref, out_ref,
    held, index_all, trace_all, picks, work, local_sem,
    xs, xr, ys, yr, ps, pr, ss, sr,
):
    gx, gy, pa = lax.axis_index("gx"), lax.axis_index("gy"), lax.axis_index("pa")
    half, vert = gx % 2, gy % 2
    xpeer = {"gx": gx + 1 - 2 * half}
    ypeer = {"gy": gy + 1 - 2 * vert}
    dpeer = {"gx": gx + 1 - 2 * half, "gy": gy + 1 - 2 * vert}
    cpeer = {"pa": 1 - pa}
    panel, width = leaf_ref.shape[1], leaf_ref.shape[2]
    step = panel // CHUNKS

    barrier = pltpu.get_barrier_semaphore()
    for peer in (xpeer, ypeer, dpeer, cpeer):
        pl.semaphore_signal(barrier, inc=1, device_id=peer, device_id_type=MESH)
    pl.semaphore_wait(barrier, 4)

    def send(src, dst, ssem, rsem, peer):
        copy = pltpu.make_async_remote_copy(
            src_ref=src, dst_ref=dst, send_sem=ssem, recv_sem=rsem,
            device_id=peer, device_id_type=MESH,
        )
        copy.start()
        return copy

    def part(rel, k):
        return held.at[rel, pa, :, pl.ds(k * step, step), :]

    small = []
    for n, peer in ((1, xpeer), (2, ypeer), (3, dpeer)):
        small.append(send(index_ref, index_all.at[n], ss.at[0, n], sr.at[0, n], peer))
        small.append(send(trace_ref, trace_all.at[n], ss.at[1, n], sr.at[1, n], peer))
    xorder = list(range(CHUNKS))
    yorder = [(k + CHUNKS // 2) % CHUNKS for k in xorder]
    xcopy, ycopy = {}, {}
    for kx, ky in zip(xorder, yorder):
        xcopy[kx] = send(leaf_ref.at[:, pl.ds(kx * step, step), :], part(1, kx), xs.at[0, kx], xr.at[0, kx], xpeer)
        ycopy[ky] = send(leaf_ref.at[:, pl.ds(ky * step, step), :], part(2, ky), ys.at[0, ky], yr.at[0, ky], ypeer)
    own = pltpu.make_async_copy(leaf_ref, held.at[0, pa], local_sem)
    own.start()
    shared = [send(leaf_ref, held.at[0, pa], ps.at[0, 0], pr.at[0, 0], cpeer)]

    index_all[0] = index_ref[...]
    trace_all[0] = trace_ref[...]
    for copy in small:
        copy.wait_recv()
    for role in range(4):
        picks[role] = one_hot(index_all[role_ref[role]], width)

    def share(rel, k):
        shared.append(send(part(rel, k), part(rel, k), ps.at[rel, k], pr.at[rel, k], cpeer))

    xfwd, yfwd = {}, {}
    for kx, ky in zip(xorder, yorder):
        xcopy[kx].wait_recv()
        if kx < CHUNKS // 2:
            yfwd[kx] = send(part(1, kx), part(3, kx), ys.at[1, kx], yr.at[1, kx], ypeer)
        share(1, kx)
        ycopy[ky].wait_recv()
        if ky >= CHUNKS // 2:
            xfwd[ky] = send(part(2, ky), part(3, ky), xs.at[1, ky], xr.at[1, ky], xpeer)
        share(2, ky)
    for ky, kx in zip(yfwd, xfwd):
        yfwd[ky].wait_recv()
        share(3, ky)
        xfwd[kx].wait_recv()
        share(3, kx)
    own.wait()
    for copy in shared:
        copy.wait_recv()

    rows = map_ref.shape[1]
    first = pl.multiple_of(half * (2 * rows) + vert * rows, rows)
    lead = role_ref[0]
    work[0, :rows] = held[lead, pa, 0, pl.ds(first, rows), :]
    work[0, rows:] = held[lead, pa, 1, pl.ds(first, rows), :]

    def pick(src, dst, role):
        value = jnp.dot(work[src], picks[role], preferred_element_type=jnp.float32)
        work[dst] = value.astype(jnp.bfloat16)

    tile = 256

    def times(src, dst, role):
        which = role_ref[role]
        left = work[src]

        @pl.loop(0, width // tile)
        def _(n):
            cols = pl.ds(pl.multiple_of(n * tile, tile), tile)
            by = []
            for c in range(2):
                total = jnp.dot(left[:, :panel], held[which, 0, c, :, cols], preferred_element_type=jnp.float32)
                total += jnp.dot(left[:, panel:], held[which, 1, c, :, cols], preferred_element_type=jnp.float32)
                by.append(total)
            real = by[0][:rows] - by[1][rows:]
            imag = by[1][:rows] + by[0][rows:]
            work[dst, :rows, cols] = real.astype(jnp.bfloat16)
            work[dst, rows:, cols] = imag.astype(jnp.bfloat16)

    pick(0, 1, 0)
    times(1, 0, 1)
    pick(0, 1, 1)
    times(1, 0, 2)
    pick(0, 1, 2)
    times(1, 0, 3)
    pick(0, 1, 3)
    map_ref[0] = work[1, :rows]
    map_ref[1] = work[1, rows:]
    trace = (trace_all[0] + trace_all[1]) + (trace_all[2] + trace_all[3])
    wide = work[1].astype(jnp.float32)
    dims = (((1,), (1,)), ((), ()))
    sums = lax.dot_general(trace, wide, dims, precision=lax.Precision.HIGHEST, preferred_element_type=jnp.float32)
    out_ref[0:1] = sums[0:1, :rows] - sums[1:2, rows:]
    out_ref[1:2] = sums[1:2, :rows] + sums[0:1, rows:]

    for copy in small + list(xcopy.values()) + list(ycopy.values()) + list(xfwd.values()) + list(yfwd.values()) + shared:
        copy.wait_send()


def per_device(leaf_maps, face_index, order_x, order_y, traces):
    leaf = leaf_maps[0, 0]
    _, panel, width = leaf.shape
    rows = panel // 4
    gx, gy = lax.axis_index("gx"), lax.axis_index("gy")
    half, vert = gx % 2, gy % 2
    base = gy // 2 * 2
    right2 = order_y[gx // 2, gy // 2]
    left2 = 1 - right2
    bit_left = order_x[gx // 2, base + left2]
    bit_right = order_x[gx // 2, base + right2]

    def rel(h, v):
        return (h ^ half) + 2 * (v ^ vert)

    roles = jnp.stack([
        rel(1 - bit_left, left2), rel(bit_left, left2),
        rel(1 - bit_right, right2), rel(bit_right, right2),
    ]).astype(jnp.int32)
    vmem = pl.BlockSpec(memory_space=pltpu.VMEM)
    dma = pltpu.SemaphoreType.DMA
    merged, outgoing = pl.pallas_call(
        kernel,
        out_shape=(
            jax.ShapeDtypeStruct((2, rows, width), jnp.bfloat16),
            jax.ShapeDtypeStruct((2, rows), jnp.float32),
        ),
        in_specs=[
            pl.BlockSpec(memory_space=pltpu.SMEM),
            pl.BlockSpec(memory_space=pl.ANY),
            vmem, vmem,
        ],
        out_specs=(vmem, vmem),
        scratch_shapes=[
            pltpu.VMEM((4, 2, 2, panel, width), jnp.bfloat16),
            pltpu.VMEM((4, 1, width), jnp.int32),
            pltpu.VMEM((4, 2, width), jnp.float32),
            pltpu.VMEM((4, width, width), jnp.bfloat16),
            pltpu.VMEM((2, 2 * rows, width), jnp.bfloat16),
            dma(()),
            dma((2, CHUNKS)), dma((2, CHUNKS)),
            dma((2, CHUNKS)), dma((2, CHUNKS)),
            dma((4, CHUNKS)), dma((4, CHUNKS)),
            dma((2, 4)), dma((2, 4)),
        ],
        compiler_params=pltpu.CompilerParams(
            collective_id=0, has_side_effects=True, vmem_limit_bytes=48 * 1024 * 1024
        ),
    )(roles, leaf, face_index[0], traces[0, 0])
    return (
        merged.reshape(1, 1, 1, 2, rows, width),
        outgoing.reshape(1, 1, 1, 2, rows),
    )


def solution(mesh):
    placed = (
        P("gx", "gy", None, "pa", None),
        P("gx", "gy", None),
        P(),
        P(),
        P("gx", "gy", None, None),
    )
    return jax.shard_map(
        per_device,
        mesh=mesh,
        in_specs=placed,
        out_specs=(P("gx", "gy", "pa", None, None, None), P("gx", "gy", "pa", None, None)),
        check_vma=False,
    )
```

time: 208 us -> 98.5 us (0.47)
  waiting for transfers between devices: 114 us -> 0 us
  Pallas kernels: 0 us -> 85.1 us
  local copies, waits for them, and re-layouts: 30.4 us -> 6.88 us
  other arithmetic: 22.3 us -> 0.08 us
  between operations: 15.6 us -> 5.25 us
  starting transfers between devices: 9.77 us -> 0 us
  matrix products: 9.28 us -> 0 us
  blocking collectives: 5.37 us -> 0 us
    ppermute x5 -> x0, waiting for transfers between devices: 94.2 us -> none  [from_partner(): return lax.ppermute(value, axis, pairs)]
    pallas_call x0 -> x1, Pallas kernels: none -> 85.1 us  [per_device(): pl.pallas_call(kernel, out_shape=(jax.ShapeDtypeStruct((2, rows, width),...]
    select_n x7 -> x0, other arithmetic: 15 us -> none  [the longest x1 5.96 us: per_device(): right_panel = jnp.where(half_index == first_bit, own_panel, sibling)]
    reduce_scatter x1 -> x0, waiting for transfers between devices: 13.6 us -> none  [per_device(): lax.psum_scatter(jnp.concatenate([real_part, imag_part], axis=1), 'pa', s...]
    slice x4 -> x0, local copies, waits for them, and re-layouts: 12.1 us -> none  [the longest x2 8.47 us: complex_rows(): right_block[1]]
    ppermute x5 -> x0, starting transfers between devices: 9.69 us -> none  [from_partner(): return lax.ppermute(value, axis, pairs)]
    dot_general x12 -> x0, matrix products: 9.28 us -> none  [the longest x2 2.91 us: complex_rows(): jnp.dot(left_block[1], right_block[0], preferred_element_type=jnp.float32)]
    gather x1 -> x0, local copies, waits for them, and re-layouts: 7.46 us -> none  [per_device(): own_panel = jnp.take(leaf_maps[0, 0], face_index[0, 0], axis=2)]
  transfers between devices with their start and end apart: 7 -> 0, of which waited for: 7 -> 0; matrix products, arithmetic and copies ran while one was open for 1% -> 0% of each run, Pallas kernels for 0% -> 0%
where the time goes in v1:
time: 98.5 us; the launch traced here: 97.3 us
  Pallas kernels  85.1 us (86%)
  local copies, waits for them, and re-layouts  6.88 us (7%)
  between operations  5.25 us (5%)
    pallas_call x1, Pallas kernels, per_device(): pl.pallas_call(kernel, out_shape=(jax.ShapeDtypeStruct((2, rows, width),...  85.1 us
    unnamed x10, local copies, waits for them, and re-layouts  4.94 us

profile of v1, /device:TPU:0, one launch (start us, length us, event | category | flops | bytes accessed | tf_op | source)
XLA Modules:
  0.0 97.3 jit_solution(5544307316625702703)
XLA Ops:
  0.6 0.0 copy-start
  0.7 0.6 copy-done
  1.3 0.6 constant_dynamic-slice_fusion
  3.8 1.4 %fusion = (s32[1,1]{0,1:T(1,128)}, s32[1,1]{0,1:T(1,128)}) fusion(s32[4,2]{0,1:T(2,128)} %param.7, s32[]{:T(128)S(6)} %select_n.34, s32[]{:T(128)S(6)} %select_n.36, s32[]{:T(128)S(6)} %select_n.39), kind=kLoop, calls=%fused_computation.2 | loop fusion | bytes 28 | tf_op jit(solution)/shard_map/dynamic_slice | solution.py:150
  7.8 0.1 pad_add_fusion.role_ref
  7.9 0.0 copy-start.1
  7.9 1.6 %copy-done.1 = bf16[1,1,2,512,1024]{4,3,2,1,0:T(8,128)(2,1)S(1)} copy-done((bf16[1,1,2,512,1024]{4,3,2,1,0:T(8,128)(2,1)S(1)}, bf16[1,1,2,512,1024]{4,3,2,1,0:T(8,128)(2,1)}, u32[]{:S(2)}) %copy-start.1) | copy-done | bytes 2097176
  9.5 0.0 copy-start.2
  9.5 0.7 copy-done.2
  10.1 0.0 copy-start.3
  10.2 0.7 copy-done.3
  10.8 85.1 %shard_map.68 = (bf16[2,128,1024]{2,1,0:T(8,128)(2,1)S(1)}, f32[2,128]{1,0:T(2,128)S(1)}) custom-call(s32[4]{0:T(128)S(1)} %pad_add_fusion.role_ref, bf16[2,512,1024]{2,1,0:T(8,128)(2,1)S(1)} %bitcast.12, s32[1,1024]{1,0:T(1,128)S(1)} %bitcast.15, f32[2,1024]{1,0:T(2,128)S(1)} %bitcast.14), custom_call_target="tpu_custom_call" | custom-call | tf_op jit(solution)/shard_map/pallas_call | solution.py:162
  95.9 0.8 copy.9
  96.7 0.6 copy.10
Async XLA Ops:
  0.6 0.7 copy-start
  7.9 1.6 %copy-start.1 = (bf16[1,1,2,512,1024]{4,3,2,1,0:T(8,128)(2,1)S(1)}, bf16[1,1,2,512,1024]{4,3,2,1,0:T(8,128)(2,1)}, u32[]{:S(2)}) copy-start(bf16[1,1,2,512,1024]{4,3,2,1,0:T(8,128)(2,1)} %param.5) | copy-start | bytes 6291460
  9.5 0.7 copy-start.2
  10.1 0.7 copy-start.3

commit v2 on v1

v2 whole, which is shorter than its diff:
```python
import jax
import jax.numpy as jnp
from jax import lax
from jax.experimental import pallas as pl
from jax.experimental.pallas import tpu as pltpu
from jax.sharding import PartitionSpec as P

MESH = pl.DeviceIdType.MESH
CHUNKS = 8
TILE = 256


def kernel(
    order_x_ref, order_y_ref, leaf_ref, index_ref, trace_ref, map_ref, out_ref,
    held, raw, index_own, pick, trace_all, work, local_sem,
    xs, xr, ys, yr, ps, pr, ss, sr,
):
    gx, gy, pa = lax.axis_index("gx"), lax.axis_index("gy"), lax.axis_index("pa")
    half, vert = gx % 2, gy % 2
    xpeer = {"gx": gx + 1 - 2 * half}
    ypeer = {"gy": gy + 1 - 2 * vert}
    dpeer = {"gx": gx + 1 - 2 * half, "gy": gy + 1 - 2 * vert}
    cpeer = {"pa": 1 - pa}
    panel, width = leaf_ref.shape[1], leaf_ref.shape[2]
    step = panel // CHUNKS
    rows = map_ref.shape[1]

    barrier = pltpu.get_barrier_semaphore()
    for peer in (xpeer, ypeer, dpeer, cpeer):
        pl.semaphore_signal(barrier, inc=1, device_id=peer, device_id_type=MESH)

    load_index = pltpu.make_async_copy(index_ref, index_own, local_sem.at[0])
    load_index.start()
    load_leaf = pltpu.make_async_copy(leaf_ref, raw, local_sem.at[1])
    load_leaf.start()
    load_trace = pltpu.make_async_copy(trace_ref, trace_all.at[0], local_sem.at[2])
    load_trace.start()

    def send(src, dst, ssem, rsem, peer):
        copy = pltpu.make_async_remote_copy(
            src_ref=src, dst_ref=dst, send_sem=ssem, recv_sem=rsem,
            device_id=peer, device_id_type=MESH,
        )
        copy.start()
        return copy

    def part(rel, k):
        return held.at[rel, :, pl.ds(pl.multiple_of(pa * panel + k * step, step), step), :]

    load_index.wait()
    index_row = index_own[...]
    grain = 256
    for n in range(width // grain):
        places = lax.broadcasted_iota(jnp.int32, (grain, width), 0) + n * grain
        pick[n * grain : (n + 1) * grain] = (places == index_row).astype(jnp.float32).astype(jnp.bfloat16)
    load_leaf.wait()

    def permute(k):
        chunk = raw[:, k * step : (k + 1) * step, :].reshape(2 * step, width)
        value = jnp.dot(chunk, pick[...], preferred_element_type=jnp.float32).astype(jnp.bfloat16)
        held[0, :, pl.ds(pl.multiple_of(pa * panel + k * step, step), step), :] = value.reshape(2, step, width)

    xorder = list(range(CHUNKS))
    yorder = [(k + CHUNKS // 2) % CHUNKS for k in xorder]
    xcopy, ycopy = {}, {}

    def send_x(k):
        xcopy[k] = send(part(0, k), part(1, k), xs.at[0, k], xr.at[0, k], xpeer)

    def send_y(k):
        ycopy[k] = send(part(0, k), part(2, k), ys.at[0, k], yr.at[0, k], ypeer)

    middle = CHUNKS // 2
    permute(0)
    permute(middle)
    pl.semaphore_wait(barrier, 4)
    for k in range(1, middle):
        send_x(k - 1)
        send_y(k - 1 + middle)
        permute(k)
        permute(k + middle)
    send_x(middle - 1)
    send_y(CHUNKS - 1)
    for k in range(middle):
        send_x(k + middle)
        send_y(k)
    own = held.at[0, :, pl.ds(pl.multiple_of(pa * panel, panel), panel), :]
    shared = [send(own, own, ps.at[0, 0], pr.at[0, 0], cpeer)]
    small = []
    for n, peer in ((1, xpeer), (2, ypeer), (3, dpeer)):
        small.append(send(trace_ref, trace_all.at[n], ss.at[n], sr.at[n], peer))

    def share(rel, k):
        shared.append(send(part(rel, k), part(rel, k), ps.at[rel, k], pr.at[rel, k], cpeer))

    xfwd, yfwd = {}, {}
    for kx, ky in zip(xorder, yorder):
        xcopy[kx].wait_recv()
        if kx < middle:
            yfwd[kx] = send(part(1, kx), part(3, kx), ys.at[1, kx], yr.at[1, kx], ypeer)
        share(1, kx)
        ycopy[ky].wait_recv()
        if ky >= middle:
            xfwd[ky] = send(part(2, ky), part(3, ky), xs.at[1, ky], xr.at[1, ky], xpeer)
        share(2, ky)
    for ky, kx in zip(yfwd, xfwd):
        yfwd[ky].wait_recv()
        share(3, ky)
        xfwd[kx].wait_recv()
        share(3, kx)
    load_trace.wait()
    for copy in small + shared:
        copy.wait_recv()

    pair, base = gx // 2, gy - vert
    right2 = order_y_ref[gy // 2, pair]
    left2 = 1 - right2
    bit_left = order_x_ref[base + left2, pair]
    bit_right = order_x_ref[base + right2, pair]

    def slot(h, v):
        return (h + half) % 2 + 2 * ((v + vert) % 2)

    first = pl.multiple_of(pa * panel + half * (2 * rows) + vert * rows, rows)
    lead = slot(1 - bit_left, left2)
    work[0, :rows] = held[lead, 0, pl.ds(first, rows), :]
    work[0, rows:] = held[lead, 1, pl.ds(first, rows), :]

    def times(src, dst, which):
        left = work[src]
        for n in range(width // TILE):
            cols = slice(n * TILE, (n + 1) * TILE)
            by = [jnp.dot(left, held[which, c, :, cols], preferred_element_type=jnp.float32) for c in range(2)]
            work[dst, :rows, cols] = (by[0][:rows] - by[1][rows:]).astype(jnp.bfloat16)
            work[dst, rows:, cols] = (by[1][:rows] + by[0][rows:]).astype(jnp.bfloat16)

    times(0, 1, slot(bit_left, left2))
    times(1, 0, slot(1 - bit_right, right2))
    times(0, 1, slot(bit_right, right2))
    map_ref[0] = work[1, :rows]
    map_ref[1] = work[1, rows:]
    trace = (trace_all[0] + trace_all[1]) + (trace_all[2] + trace_all[3])
    wide = work[1].astype(jnp.float32)
    ones = jnp.ones((8, 128), jnp.float32)
    dims = (((1,), (1,)), ((), ()))
    sums = []
    for c in range(2):
        scaled = wide * trace[c : c + 1]
        folded = scaled[:, :128]
        for n in range(1, width // 128):
            folded += scaled[:, n * 128 : (n + 1) * 128]
        sums.append(lax.dot_general(ones, folded, dims, precision=lax.Precision.HIGHEST, preferred_element_type=jnp.float32))
    out_ref[0:1] = sums[0][0:1, :rows] - sums[1][0:1, rows:]
    out_ref[1:2] = sums[1][0:1, :rows] + sums[0][0:1, rows:]

    for copy in small + list(xcopy.values()) + list(ycopy.values()) + list(xfwd.values()) + list(yfwd.values()) + shared:
        copy.wait_send()


def per_device(leaf_maps, face_index, order_x, order_y, traces):
    leaf = leaf_maps[0, 0]
    _, panel, width = leaf.shape
    rows = panel // 4
    vmem = pl.BlockSpec(memory_space=pltpu.VMEM)
    smem = pl.BlockSpec(memory_space=pltpu.SMEM)
    hbm = pl.BlockSpec(memory_space=pl.ANY)
    dma = pltpu.SemaphoreType.DMA
    merged, outgoing = pl.pallas_call(
        kernel,
        out_shape=(
            jax.ShapeDtypeStruct((2, rows, width), jnp.bfloat16),
            jax.ShapeDtypeStruct((2, rows), jnp.float32),
        ),
        in_specs=[smem, smem, hbm, hbm, hbm],
        out_specs=(vmem, vmem),
        scratch_shapes=[
            pltpu.VMEM((4, 2, 2 * panel, width), jnp.bfloat16),
            pltpu.VMEM((2, panel, width), jnp.bfloat16),
            pltpu.VMEM((1, width), jnp.int32),
            pltpu.VMEM((width, width), jnp.bfloat16),
            pltpu.VMEM((4, 2, width), jnp.float32),
            pltpu.VMEM((2, 2 * rows, width), jnp.bfloat16),
            dma((3,)),
            dma((2, CHUNKS)), dma((2, CHUNKS)),
            dma((2, CHUNKS)), dma((2, CHUNKS)),
            dma((4, CHUNKS)), dma((4, CHUNKS)),
            dma((4,)), dma((4,)),
        ],
        compiler_params=pltpu.CompilerParams(
            collective_id=0, has_side_effects=True, vmem_limit_bytes=67043328
        ),
    )(order_x.T, order_y.T, leaf, face_index[0], traces[0, 0])
    return (
        merged.reshape(1, 1, 1, 2, rows, width),
        outgoing.reshape(1, 1, 1, 2, rows),
    )


def solution(mesh):
    placed = (
        P("gx", "gy", None, "pa", None),
        P("gx", "gy", None),
        P(),
        P(),
        P("gx", "gy", None, None),
    )
    return jax.shard_map(
        per_device,
        mesh=mesh,
        in_specs=placed,
        out_specs=(P("gx", "gy", "pa", None, None, None), P("gx", "gy", "pa", None, None)),
        check_vma=False,
    )
```

time: 98.5 us -> 85.8 us (0.87)
  between operations: 5.25 us -> 0.64 us
  Pallas kernels: 85.1 us -> 81.2 us
  local copies, waits for them, and re-layouts: 6.88 us -> 3.07 us
    pallas_call x1, Pallas kernels: 85.1 us -> 81.2 us  [per_device(): pl.pallas_call(kernel, out_shape=(jax.ShapeDtypeStruct((2, rows, width),...]
    dynamic_slice x2 -> x0, local copies, waits for them, and re-layouts: 1.93 us -> none  [the longest x1 1.35 us: per_device(): bit_left = order_x[gx // 2, base + left2]]
    unnamed x10 -> x2, local copies, waits for them, and re-layouts: 4.94 us -> 3.07 us
where the time goes in v2:
time: 85.8 us; the launch traced here: 84.9 us
  Pallas kernels  81.2 us (95%)
  local copies, waits for them, and re-layouts  3.07 us (4%)
    pallas_call x1, Pallas kernels, per_device(): pl.pallas_call(kernel, out_shape=(jax.ShapeDtypeStruct((2, rows, width),...  81.2 us
    unnamed x2, local copies, waits for them, and re-layouts  3.07 us

profile of v2, /device:TPU:0, one launch (start us, length us, event | category | flops | bytes accessed | tf_op | source)
XLA Modules:
  0.0 84.9 jit_solution(16518864619277327498)
XLA Ops:
  0.6 81.2 %shard_map.68 = (bf16[2,128,1024]{2,1,0:T(8,128)(2,1)}, f32[2,128]{1,0:T(2,128)}) custom-call(s32[2,4]{1,0:T(2,128)} %bitcast.11, s32[1,4]{1,0:T(1,128)} %bitcast.13, bf16[2,512,1024]{2,1,0:T(8,128)(2,1)} %bitcast.7, s32[1,1024]{1,0:T(1,128)} %bitcast.10, f32[2,1024]{1,0:T(2,128)} %bitcast.9), custom_call_target="tpu_custom_call" | custom-call | tf_op jit(solution)/shard_map/pallas_call | solution.py:168
  81.8 1.9 %copy.9 = bf16[1,1,1,2,128,1024]{5,4,3,2,1,0:T(8,128)(2,1)} copy(bf16[1,1,1,2,128,1024]{5,4,3,2,1,0:T(8,128)(2,1)} %bitcast.8) | data formatting | bytes 1048576
  83.7 1.2 %copy.10 = f32[1,1,1,2,128]{4,3,2,1,0:T(2,128)} copy(f32[1,1,1,2,128]{4,3,2,1,0:T(2,128)} %bitcast.12) | data formatting | bytes 2048

commit v3 on v2

--- a/solution.py
+++ b/solution.py
@@ -12,7 +12,8 @@
 
 def kernel(
     order_x_ref, order_y_ref, leaf_ref, index_ref, trace_ref, map_ref, out_ref,
-    held, raw, index_own, pick, trace_all, work, local_sem,
+    held, raw, index_own, pick, trace_all, work, ask, ask_in, reply, reply_in,
+    local_sem,
     xs, xr, ys, yr, ps, pr, ss, sr,
 ):
     gx, gy, pa = lax.axis_index("gx"), lax.axis_index("gy"), lax.axis_index("pa")
@@ -60,30 +61,20 @@
         value = jnp.dot(chunk, pick[...], preferred_element_type=jnp.float32).astype(jnp.bfloat16)
         held[0, :, pl.ds(pl.multiple_of(pa * panel + k * step, step), step), :] = value.reshape(2, step, width)
 
-    xorder = list(range(CHUNKS))
-    yorder = [(k + CHUNKS // 2) % CHUNKS for k in xorder]
     xcopy, ycopy = {}, {}
 
-    def send_x(k):
-        xcopy[k] = send(part(0, k), part(1, k), xs.at[0, k], xr.at[0, k], xpeer)
-
-    def send_y(k):
-        ycopy[k] = send(part(0, k), part(2, k), ys.at[0, k], yr.at[0, k], ypeer)
-
-    middle = CHUNKS // 2
+    def send_both(k):
+        xcopy[k] = send(part(0, k), part(1, k), xs.at[k], xr.at[k], xpeer)
+        ycopy[k] = send(part(0, k), part(2, k), ys.at[k], yr.at[k], ypeer)
+
     permute(0)
-    permute(middle)
+    permute(1)
     pl.semaphore_wait(barrier, 4)
-    for k in range(1, middle):
-        send_x(k - 1)
-        send_y(k - 1 + middle)
+    for k in range(2, CHUNKS):
+        send_both(k - 2)
         permute(k)
-        permute(k + middle)
-    send_x(middle - 1)
-    send_y(CHUNKS - 1)
-    for k in range(middle):
-        send_x(k + middle)
-        send_y(k)
+    send_both(CHUNKS - 2)
+    send_both(CHUNKS - 1)
     own = held.at[0, :, pl.ds(pl.multiple_of(pa * panel, panel), panel), :]
     shared = [send(own, own, ps.at[0, 0], pr.at[0, 0], cpeer)]
     small = []
@@ -93,21 +84,11 @@
     def share(rel, k):
         shared.append(send(part(rel, k), part(rel, k), ps.at[rel, k], pr.at[rel, k], cpeer))
 
-    xfwd, yfwd = {}, {}
-    for kx, ky in zip(xorder, yorder):
-        xcopy[kx].wait_recv()
-        if kx < middle:
-            yfwd[kx] = send(part(1, kx), part(3, kx), ys.at[1, kx], yr.at[1, kx], ypeer)
-        share(1, kx)
-        ycopy[ky].wait_recv()
-        if ky >= middle:
-            xfwd[ky] = send(part(2, ky), part(3, ky), xs.at[1, ky], xr.at[1, ky], xpeer)
-        share(2, ky)
-    for ky, kx in zip(yfwd, xfwd):
-        yfwd[ky].wait_recv()
-        share(3, ky)
-        xfwd[kx].wait_recv()
-        share(3, kx)
+    for k in range(CHUNKS):
+        xcopy[k].wait_recv()
+        share(1, k)
+        ycopy[k].wait_recv()
+        share(2, k)
     load_trace.wait()
     for copy in small + shared:
         copy.wait_recv()
@@ -121,26 +102,44 @@
     def slot(h, v):
         return (h + half) % 2 + 2 * ((v + vert) % 2)
 
+    slots = [
+        slot(1 - bit_left, left2), slot(bit_left, left2),
+        slot(1 - bit_right, right2), slot(bit_right, right2),
+    ]
+    here = [jnp.minimum(which, 2) for which in slots]
     first = pl.multiple_of(pa * panel + half * (2 * rows) + vert * rows, rows)
-    lead = slot(1 - bit_left, left2)
-    work[0, :rows] = held[lead, 0, pl.ds(first, rows), :]
-    work[0, rows:] = held[lead, 1, pl.ds(first, rows), :]
-
-    def times(src, dst, which):
-        left = work[src]
+
+    def times(src, dst, which, use=None):
+        left = src[...].reshape(2 * rows, width)
         for n in range(width // TILE):
             cols = slice(n * TILE, (n + 1) * TILE)
             by = [jnp.dot(left, held[which, c, :, cols], preferred_element_type=jnp.float32) for c in range(2)]
-            work[dst, :rows, cols] = (by[0][:rows] - by[1][rows:]).astype(jnp.bfloat16)
-            work[dst, rows:, cols] = (by[1][:rows] + by[0][rows:]).astype(jnp.bfloat16)
-
-    times(0, 1, slot(bit_left, left2))
-    times(1, 0, slot(1 - bit_right, right2))
-    times(0, 1, slot(bit_right, right2))
-    map_ref[0] = work[1, :rows]
-    map_ref[1] = work[1, rows:]
+            real = (by[0][:rows] - by[1][rows:]).astype(jnp.bfloat16)
+            imag = (by[1][:rows] + by[0][rows:]).astype(jnp.bfloat16)
+            if use is not None:
+                real = jnp.where(use, real, src[0, :, cols])
+                imag = jnp.where(use, imag, src[1, :, cols])
+            dst[0, :, cols] = real
+            dst[1, :, cols] = imag
+
+    spot = lax.broadcasted_iota(jnp.int32, (rows, width), 0) + first
+    unit = (lax.broadcasted_iota(jnp.int32, (rows, width), 1) == spot).astype(jnp.float32).astype(jnp.bfloat16)
+    away = slots[0] == 3
+    work[0, 0] = jnp.where(away, unit, held[here[0], 0, pl.ds(first, rows), :])
+    work[0, 1] = jnp.where(away, jnp.zeros_like(unit), held[here[0], 1, pl.ds(first, rows), :])
+    times(work.at[0], work.at[1], here[1], slots[2] // 3 + slots[3] // 3 > 0)
+    times(work.at[1], ask, here[2], slots[3] == 3)
+    peer = {"gx": gx + (1 - 2 * half) * (1 - pa), "gy": gy + (1 - 2 * vert) * pa}
+    asked = send(ask, ask_in, ss.at[0], sr.at[0], peer)
+    asked.wait_recv()
+    times(ask_in, reply, 2 - pa)
+    replied = send(reply, reply_in, ss.at[4], sr.at[4], peer)
+    replied.wait_recv()
+    times(reply_in, work.at[0], here[1], away)
+    times(work.at[0], work.at[1], here[2], slots[0] // 3 + slots[1] // 3 > 0)
+    times(work.at[1], map_ref, here[3], slots[3] != 3)
     trace = (trace_all[0] + trace_all[1]) + (trace_all[2] + trace_all[3])
-    wide = work[1].astype(jnp.float32)
+    wide = map_ref[...].reshape(2 * rows, width).astype(jnp.float32)
     ones = jnp.ones((8, 128), jnp.float32)
     dims = (((1,), (1,)), ((), ()))
     sums = []
@@ -153,7 +152,7 @@
     out_ref[0:1] = sums[0][0:1, :rows] - sums[1][0:1, rows:]
     out_ref[1:2] = sums[1][0:1, :rows] + sums[0][0:1, rows:]
 
-    for copy in small + list(xcopy.values()) + list(ycopy.values()) + list(xfwd.values()) + list(yfwd.values()) + shared:
+    for copy in small + list(xcopy.values()) + list(ycopy.values()) + shared + [asked, replied]:
         copy.wait_send()
 
 
@@ -174,17 +173,21 @@
         in_specs=[smem, smem, hbm, hbm, hbm],
         out_specs=(vmem, vmem),
         scratch_shapes=[
-            pltpu.VMEM((4, 2, 2 * panel, width), jnp.bfloat16),
+            pltpu.VMEM((3, 2, 2 * panel, width), jnp.bfloat16),
             pltpu.VMEM((2, panel, width), jnp.bfloat16),
             pltpu.VMEM((1, width), jnp.int32),
             pltpu.VMEM((width, width), jnp.bfloat16),
             pltpu.VMEM((4, 2, width), jnp.float32),
-            pltpu.VMEM((2, 2 * rows, width), jnp.bfloat16),
+            pltpu.VMEM((2, 2, rows, width), jnp.bfloat16),
+            pltpu.VMEM((2, rows, width), jnp.bfloat16),
+            pltpu.VMEM((2, rows, width), jnp.bfloat16),
+            pltpu.VMEM((2, rows, width), jnp.bfloat16),
+            pltpu.VMEM((2, rows, width), jnp.bfloat16),
             dma((3,)),
-            dma((2, CHUNKS)), dma((2, CHUNKS)),
-            dma((2, CHUNKS)), dma((2, CHUNKS)),
-            dma((4, CHUNKS)), dma((4, CHUNKS)),
-            dma((4,)), dma((4,)),
+            dma((CHUNKS,)), dma((CHUNKS,)),
+            dma((CHUNKS,)), dma((CHUNKS,)),
+            dma((3, CHUNKS)), dma((3, CHUNKS)),
+            dma((5,)), dma((5,)),
         ],
         compiler_params=pltpu.CompilerParams(
             collective_id=0, has_side_effects=True, vmem_limit_bytes=67043328

time: 85.8 us -> 82.4 us (0.960)
  Pallas kernels: 81.2 us -> 78.5 us
    pallas_call x1, Pallas kernels: 81.2 us -> 78.5 us  [per_device(): pl.pallas_call(kernel, out_shape=(jax.ShapeDtypeStruct((2, rows, width),...]
where the time goes in v3:
time: 82.4 us; the launch traced here: 82.2 us
  Pallas kernels  78.5 us (95%)
  local copies, waits for them, and re-layouts  3.07 us (4%)
    pallas_call x1, Pallas kernels, per_device(): pl.pallas_call(kernel, out_shape=(jax.ShapeDtypeStruct((2, rows, width),...  78.5 us
    unnamed x2, local copies, waits for them, and re-layouts  3.07 us

profile of v3, /device:TPU:0, one launch (start us, length us, event | category | flops | bytes accessed | tf_op | source)
XLA Modules:
  0.0 82.2 jit_solution(9033436314085250119)
XLA Ops:
  0.6 78.5 %shard_map.68 = (bf16[2,128,1024]{2,1,0:T(8,128)(2,1)}, f32[2,128]{1,0:T(2,128)}) custom-call(s32[2,4]{1,0:T(2,128)} %bitcast.11, s32[1,4]{1,0:T(1,128)} %bitcast.13, bf16[2,512,1024]{2,1,0:T(8,128)(2,1)} %bitcast.7, s32[1,1024]{1,0:T(1,128)} %bitcast.10, f32[2,1024]{1,0:T(2,128)} %bitcast.9), custom_call_target="tpu_custom_call" | custom-call | tf_op jit(solution)/shard_map/pallas_call | solution.py:167
  79.1 1.9 %copy.9 = bf16[1,1,1,2,128,1024]{5,4,3,2,1,0:T(8,128)(2,1)} copy(bf16[1,1,1,2,128,1024]{5,4,3,2,1,0:T(8,128)(2,1)} %bitcast.8) | data formatting | bytes 1048576
  81.0 1.2 %copy.10 = f32[1,1,1,2,128]{4,3,2,1,0:T(2,128)} copy(f32[1,1,1,2,128]{4,3,2,1,0:T(2,128)} %bitcast.12) | data formatting | bytes 2048

commit v4 on v3

--- a/solution.py
+++ b/solution.py
@@ -13,8 +13,8 @@
 def kernel(
     order_x_ref, order_y_ref, leaf_ref, index_ref, trace_ref, map_ref, out_ref,
     held, raw, index_own, pick, trace_all, work, ask, ask_in, reply, reply_in,
-    local_sem,
-    xs, xr, ys, yr, ps, pr, ss, sr,
+    total, local_sem,
+    xs, xr, ys, yr, ps, pr, ss, sr, ts, tr,
 ):
     gx, gy, pa = lax.axis_index("gx"), lax.axis_index("gy"), lax.axis_index("pa")
     half, vert = gx % 2, gy % 2
@@ -109,7 +109,7 @@
     here = [jnp.minimum(which, 2) for which in slots]
     first = pl.multiple_of(pa * panel + half * (2 * rows) + vert * rows, rows)
 
-    def times(src, dst, which, use=None):
+    def times(src, dst, which, use=None, after=None):
         left = src[...].reshape(2 * rows, width)
         for n in range(width // TILE):
             cols = slice(n * TILE, (n + 1) * TILE)
@@ -121,6 +121,10 @@
                 imag = jnp.where(use, imag, src[1, :, cols])
             dst[0, :, cols] = real
             dst[1, :, cols] = imag
+            if after is not None and n:
+                after(n - 1)
+        if after is not None:
+            after(width // TILE - 1)
 
     spot = lax.broadcasted_iota(jnp.int32, (rows, width), 0) + first
     unit = (lax.broadcasted_iota(jnp.int32, (rows, width), 1) == spot).astype(jnp.float32).astype(jnp.bfloat16)
@@ -128,14 +132,49 @@
     work[0, 0] = jnp.where(away, unit, held[here[0], 0, pl.ds(first, rows), :])
     work[0, 1] = jnp.where(away, jnp.zeros_like(unit), held[here[0], 1, pl.ds(first, rows), :])
     times(work.at[0], work.at[1], here[1], slots[2] // 3 + slots[3] // 3 > 0)
-    times(work.at[1], ask, here[2], slots[3] == 3)
     peer = {"gx": gx + (1 - 2 * half) * (1 - pa), "gy": gy + (1 - 2 * vert) * pa}
-    asked = send(ask, ask_in, ss.at[0], sr.at[0], peer)
-    asked.wait_recv()
-    times(ask_in, reply, 2 - pa)
-    replied = send(reply, reply_in, ss.at[4], sr.at[4], peer)
-    replied.wait_recv()
-    times(reply_in, work.at[0], here[1], away)
+    tiles = width // TILE
+
+    def tile_of(ref, n):
+        return ref.at[:, :, n * TILE : (n + 1) * TILE]
+
+    def sender(src, dst, row, copies):
+        def after(n):
+            copies.append(send(tile_of(src, n), tile_of(dst, n), ts.at[row, n], tr.at[row, n], peer))
+        return after
+
+    def times_arriving(copies, src, dst, which, use=None, after=None):
+        for n in range(tiles):
+            deep = slice(n * TILE, (n + 1) * TILE)
+            copies[n].wait_recv()
+            left = src[:, :, deep].reshape(2 * rows, TILE)
+            for m in range(tiles):
+                cols = slice(m * TILE, (m + 1) * TILE)
+                by = []
+                for c in range(2):
+                    term = jnp.dot(left, held[which, c, deep, cols], preferred_element_type=jnp.float32)
+                    if n:
+                        term += total[c, :, cols]
+                    if n < tiles - 1:
+                        total[c, :, cols] = term
+                    by.append(term)
+                if n == tiles - 1:
+                    real = (by[0][:rows] - by[1][rows:]).astype(jnp.bfloat16)
+                    imag = (by[1][:rows] + by[0][rows:]).astype(jnp.bfloat16)
+                    if use is not None:
+                        real = jnp.where(use, real, src[0, :, cols])
+                        imag = jnp.where(use, imag, src[1, :, cols])
+                    dst[0, :, cols] = real
+                    dst[1, :, cols] = imag
+                    if after is not None and m:
+                        after(m - 1)
+        if after is not None:
+            after(tiles - 1)
+
+    asked, replied = [], []
+    times(work.at[1], ask, here[2], slots[3] == 3, sender(ask, ask_in, 0, asked))
+    times_arriving(asked, ask_in, reply, 2 - pa, None, sender(reply, reply_in, 1, replied))
+    times_arriving(replied, reply_in, work.at[0], here[1], away)
     times(work.at[0], work.at[1], here[2], slots[0] // 3 + slots[1] // 3 > 0)
     times(work.at[1], map_ref, here[3], slots[3] != 3)
     trace = (trace_all[0] + trace_all[1]) + (trace_all[2] + trace_all[3])
@@ -152,7 +191,7 @@
     out_ref[0:1] = sums[0][0:1, :rows] - sums[1][0:1, rows:]
     out_ref[1:2] = sums[1][0:1, :rows] + sums[0][0:1, rows:]
 
-    for copy in small + list(xcopy.values()) + list(ycopy.values()) + shared + [asked, replied]:
+    for copy in small + list(xcopy.values()) + list(ycopy.values()) + shared + asked + replied:
         copy.wait_send()
 
 
@@ -183,11 +222,13 @@
             pltpu.VMEM((2, rows, width), jnp.bfloat16),
             pltpu.VMEM((2, rows, width), jnp.bfloat16),
             pltpu.VMEM((2, rows, width), jnp.bfloat16),
+            pltpu.VMEM((2, 2 * rows, width), jnp.float32),
             dma((3,)),
             dma((CHUNKS,)), dma((CHUNKS,)),
             dma((CHUNKS,)), dma((CHUNKS,)),
             dma((3, CHUNKS)), dma((3, CHUNKS)),
-            dma((5,)), dma((5,)),
+            dma((4,)), dma((4,)),
+            dma((2, width // TILE)), dma((2, width // TILE)),
         ],
         compiler_params=pltpu.CompilerParams(
             collective_id=0, has_side_effects=True, vmem_limit_bytes=67043328

time: 82.4 us -> 80.2 us (0.973)
  Pallas kernels: 78.5 us -> 76.3 us
    pallas_call x1, Pallas kernels: 78.5 us -> 76.3 us  [per_device(): pl.pallas_call(kernel, out_shape=(jax.ShapeDtypeStruct((2, rows, width),...]
where the time goes in v4:
time: 80.2 us; the launch traced here: 80 us
  Pallas kernels  76.3 us (95%)
  local copies, waits for them, and re-layouts  3.07 us (4%)
    pallas_call x1, Pallas kernels, per_device(): pl.pallas_call(kernel, out_shape=(jax.ShapeDtypeStruct((2, rows, width),...  76.3 us
    unnamed x2, local copies, waits for them, and re-layouts  3.07 us

profile of v4, /device:TPU:0, one launch (start us, length us, event | category | flops | bytes accessed | tf_op | source)
XLA Modules:
  0.0 80.0 jit_solution(10788828978356501919)
XLA Ops:
  0.6 76.3 %shard_map.68 = (bf16[2,128,1024]{2,1,0:T(8,128)(2,1)}, f32[2,128]{1,0:T(2,128)}) custom-call(s32[2,4]{1,0:T(2,128)} %bitcast.11, s32[1,4]{1,0:T(1,128)} %bitcast.13, bf16[2,512,1024]{2,1,0:T(8,128)(2,1)} %bitcast.7, s32[1,1024]{1,0:T(1,128)} %bitcast.10, f32[2,1024]{1,0:T(2,128)} %bitcast.9), custom_call_target="tpu_custom_call" | custom-call | tf_op jit(solution)/shard_map/pallas_call | solution.py:206
  76.9 1.9 %copy.9 = bf16[1,1,1,2,128,1024]{5,4,3,2,1,0:T(8,128)(2,1)} copy(bf16[1,1,1,2,128,1024]{5,4,3,2,1,0:T(8,128)(2,1)} %bitcast.8) | data formatting | bytes 1048576
  78.8 1.2 %copy.10 = f32[1,1,1,2,128]{4,3,2,1,0:T(2,128)} copy(f32[1,1,1,2,128]{4,3,2,1,0:T(2,128)} %bitcast.12) | data formatting | bytes 2048

commit v5 on v4

--- a/solution.py
+++ b/solution.py
@@ -206,8 +206,8 @@
     merged, outgoing = pl.pallas_call(
         kernel,
         out_shape=(
-            jax.ShapeDtypeStruct((2, rows, width), jnp.bfloat16),
-            jax.ShapeDtypeStruct((2, rows), jnp.float32),
+            pltpu.VMEM((2, rows, width), jnp.bfloat16),
+            pltpu.VMEM((2, rows), jnp.float32),
         ),
         in_specs=[smem, smem, hbm, hbm, hbm],
         out_specs=(vmem, vmem),
@@ -231,7 +231,7 @@
             dma((2, width // TILE)), dma((2, width // TILE)),
         ],
         compiler_params=pltpu.CompilerParams(
-            collective_id=0, has_side_effects=True, vmem_limit_bytes=67043328
+            collective_id=0, has_side_effects=True, vmem_limit_bytes=60 * 1024 * 1024
         ),
     )(order_x.T, order_y.T, leaf, face_index[0], traces[0, 0])
     return (

time: 80.2 us -> 77.7 us (0.969)
  local copies, waits for them, and re-layouts: 3.07 us -> 1.36 us
    unnamed x2, local copies, waits for them, and re-layouts: 3.07 us -> 1.36 us
where the time goes in v5:
time: 77.7 us; the launch traced here: 77.5 us
  Pallas kernels  75.5 us (97%)
  local copies, waits for them, and re-layouts  1.36 us (2%)
    pallas_call x1, Pallas kernels, per_device(): pl.pallas_call(kernel, out_shape=(pltpu.VMEM((2, rows, width), jnp.bfloat...  75.5 us

profile of v5, /device:TPU:0, one launch (start us, length us, event | category | flops | bytes accessed | tf_op | source)
XLA Modules:
  0.0 77.5 jit_solution(1207282153756824533)
XLA Ops:
  0.6 75.5 %shard_map.68 = (bf16[2,128,1024]{2,1,0:T(8,128)(2,1)S(1)}, f32[2,128]{1,0:T(2,128)S(1)}) custom-call(s32[2,4]{1,0:T(2,128)} %bitcast.12, s32[1,4]{1,0:T(1,128)} %bitcast.13, bf16[2,512,1024]{2,1,0:T(8,128)(2,1)} %bitcast.9, s32[1,1024]{1,0:T(1,128)} %bitcast.11, f32[2,1024]{1,0:T(2,128)} %bitcast.10), custom_call_target="tpu_custom_call" | custom-call | tf_op jit(solution)/shard_map/pallas_call | solution.py:206
  76.1 0.8 %copy.9 = bf16[1,1,1,2,128,1024]{5,4,3,2,1,0:T(8,128)(2,1)} copy(bf16[1,1,1,2,128,1024]{5,4,3,2,1,0:T(8,128)(2,1)S(1)} %bitcast.7) | data formatting | bytes 1048576
  76.9 0.6 copy.10
